TPU v7x, 32 devices: a whole 2x2x4 slice. The times are simulated.
32 devices in a mesh: depth: 2 (over x), mode: 2 (over y), tile: 8 (over z, core).
Axes of the slice: x: 2, y: 2, z: 4, core: 2. Of those that a mesh axis runs over, the one named last changes fastest.
Arguments:
- probe: float32 [2, 2, 256, 256], P('mode'), may hold values from -3 to 3
- object_slices: float32 [2, 2, 384, 2048], P('depth', None, None, 'tile'), may hold values from -4.2 to 4.2
- positions: int32 [16, 2], P('tile'), may hold values from 0 to 256, as said below
- measured: float32 [16, 256, 256], P('tile'), may hold values from 0 to 2
Outputs:
- object_gradient: float32 [2, 2, 384, 2048], P('depth', None, None, 'tile')
Inputs may be any that keep to these rules, and one draw needn't show every extreme that they name: `positions`: position r belongs to tile r // 2. Entry 0 is its window's first row, at most 128; entry 1 is its first column counted in the tile's columns extended by 128 on each side, at most 256. Windows never leave the object: in the first tile the column entry is at least 128, in the last at most 128.
All inputs are finite; a program needn't handle non-finite values.
Results may differ from a plain program's by a relative error of at most 0.0003.
Values sent between devices are 32-bit elements; how exact they have to be, the bound alone decides.
A program may use at most 64 MiB of HBM per device.

v0:
```python
import functools
import math

import jax
import jax.numpy as jnp
import numpy as np
from jax import lax
from jax.experimental import pallas as pl
from jax.experimental.pallas import tpu as pltpu
from jax.sharding import PartitionSpec as P

HALO = 128
MESH = pl.DeviceIdType.MESH


def split_table(table):
    high = table.astype(jnp.bfloat16)
    low = (table - high.astype(np.float64)).astype(jnp.bfloat16)
    return np.stack([high, low], 0)


def dft_tables(length):
    ordinal = np.arange(length)
    angle = 2.0 * math.pi / length * (ordinal[:, None] * ordinal[None, :] % length)
    cosine = np.cos(angle) / math.sqrt(length)
    sine = np.sin(angle) / math.sqrt(length)
    first = np.block([[cosine, -sine], [sine, cosine]])
    second = np.block([[cosine, sine], [-sine, cosine]])
    return np.stack([split_table(first), split_table(second)], 0)


def propagator(length):
    ordinal = np.arange(length)
    signed = np.where(ordinal < length - length // 2, ordinal, ordinal - length)
    square = signed[:, None] * signed[:, None] + signed[None, :] * signed[None, :]
    angle = -math.pi / (2.0 * length) * (3 * square % (4 * length))
    return np.stack([np.cos(angle), np.sin(angle)], 0).astype(np.float32)


def parts_of(value):
    high = value.astype(jnp.bfloat16)
    low = (value - high.astype(jnp.float32)).astype(jnp.bfloat16)
    return high, low


def mm(a, b):
    return jnp.dot(a, b, preferred_element_type=jnp.float32)


def transform(real, imag, tab, right, left):
    n = real.shape[0]
    high, low = parts_of(jnp.concatenate([real, imag], axis=1))
    half = mm(high, tab[right, 0]) + mm(low, tab[right, 0]) + mm(high, tab[right, 1])
    high, low = parts_of(jnp.concatenate([half[:, :n], half[:, n:]], axis=0))
    full = mm(tab[left, 0], high) + mm(tab[left, 0], low) + mm(tab[left, 1], high)
    return full[:n], full[n:]


def kernel(
    pairs,
    probe_ref,
    obj_ref,
    pos_ref,
    meas_ref,
    tab_hbm,
    prop_hbm,
    out_ref,
    ext_near,
    ext_far,
    psi0,
    psi1,
    win,
    pattern,
    posn,
    tab,
    prop,
    mine_int,
    their_int,
    vsend,
    vrecv,
    spread,
    accum,
    rim,
    load_sem,
    src_sem,
    fwd_sem,
    ext_sem,
    pos_sem,
    probe_sem,
    meas_sem,
    int_sem,
    v_sem,
    w_send,
    w_recv,
    rim_send,
    rim_recv,
    out_send,
    out_recv,
):
    n = psi0.shape[1]
    rows = obj_ref.shape[2]
    room = rows - n
    d = lax.axis_index("depth")
    m = lax.axis_index("mode")
    t = lax.axis_index("tile")
    c = lax.rem(t, 2)
    z = t // 2
    other = t + 1 - 2 * c
    own = 1 - (c - d) * (c - d)
    core = {"tile": other}
    across = {"depth": 1 - d}
    beside = {"mode": 1 - m}
    is_owner = c == d
    not_owner = c != d

    def rcopy(src, dst, send, recv, target):
        return pltpu.make_async_remote_copy(
            src_ref=src, dst_ref=dst, send_sem=send, recv_sem=recv, device_id=target, device_id_type=MESH
        )

    loads = [
        pltpu.make_async_copy(tab_hbm, tab, load_sem.at[0]),
        pltpu.make_async_copy(prop_hbm, prop, load_sem.at[1]),
    ]
    for item in loads:
        item.start()

    barrier = pltpu.get_barrier_semaphore()
    for target in (core, across, beside):
        pl.semaphore_signal(barrier, inc=1, device_id=target, device_id_type=MESH)

    @pl.when(z > 0)
    def _():
        for depth in (0, 1):
            pl.semaphore_signal(barrier, inc=1, device_id={"depth": depth, "tile": t - 2}, device_id_type=MESH)

    @pl.when(z < pairs - 1)
    def _():
        for depth in (0, 1):
            pl.semaphore_signal(barrier, inc=1, device_id={"depth": depth, "tile": t + 2}, device_id_type=MESH)

    peers = 3 + 2 * jnp.minimum(z, 1) + 2 * jnp.minimum(pairs - 1 - z, 1)
    pl.semaphore_wait(barrier, peers)

    ext = (ext_near, ext_far)

    def half_of(h):
        return obj_ref.at[0, :, :, pl.ds(pl.multiple_of(h * HALO, HALO), HALO)]

    def place(src, block, send, depth):
        for s in (0, 1):
            dst = ext[s].at[block]
            sem = ext_sem.at[s, block]

            @pl.when(jnp.logical_and(d == s, depth == s))
            def _():
                pltpu.make_async_copy(src, dst, sem).start()

            @pl.when(jnp.logical_and(d == s, depth != s))
            def _():
                rcopy(src, dst, send, sem, across).start()

    inner_block = 3 * c
    outer_block = 3 - 3 * c
    outer_tile = t - 2 + 4 * c
    has_outer = jnp.logical_or(jnp.logical_and(c == 0, z > 0), jnp.logical_and(c == 1, z < pairs - 1))

    def outer_copy(s):
        return rcopy(
            half_of(c),
            ext[s].at[outer_block],
            src_sem.at[3],
            ext_sem.at[s, outer_block],
            {"depth": 1 - c, "tile": outer_tile},
        )

    pos_copy = rcopy(pos_ref, posn, pos_sem.at[0], pos_sem.at[1], core)
    pos_copy.start()
    place(half_of(0), 1, src_sem.at[0], c)
    place(half_of(1), 2, src_sem.at[1], c)
    place(half_of(1 - c), inner_block, src_sem.at[2], 1 - c)

    for s in (0, 1):

        @pl.when(jnp.logical_and(has_outer, d == s))
        def _():
            outer_copy(s).start()

    probe_copy = rcopy(probe_ref.at[0], psi0, probe_sem.at[0], probe_sem.at[1], beside)

    @pl.when(c == m)
    def _():
        probe_copy.start()
        pltpu.make_async_copy(probe_ref.at[0], psi0, probe_sem.at[2]).start()

    meas_copy = rcopy(meas_ref.at[m], pattern, meas_sem.at[0], meas_sem.at[1], core)
    meas_local = pltpu.make_async_copy(meas_ref.at[m], pattern, meas_sem.at[2])

    @pl.when(is_owner)
    def _():
        meas_copy.start()
        meas_local.start()

    for s in (0, 1):
        ext[s][4] = jnp.zeros(ext_near.shape[1:], jnp.float32)

    no_left = jnp.logical_and(d == 0, z == 0)
    no_right = jnp.logical_and(d == 1, z == pairs - 1)

    @pl.when(no_left)
    def _():
        for s in (0, 1):
            ext[s][0] = jnp.zeros(ext_near.shape[1:], jnp.float32)

    @pl.when(no_right)
    def _():
        for s in (0, 1):
            ext[s][3] = jnp.zeros(ext_near.shape[1:], jnp.float32)

    @pl.when(is_owner)
    def _():
        @pl.loop(0, 4)
        def _(w):
            for j in (0, 1, 2, 5, 6):
                spread[w // 2, lax.rem(w, 2), j] = jnp.zeros(spread.shape[3:], jnp.float32)
            for j in (3, 4):
                for edge in (0, room + n):
                    spread[w // 2, lax.rem(w, 2), j, :, edge : edge + room, :] = jnp.zeros((2, room, HALO), jnp.float32)

    def ext_wait(s, block):
        rcopy(ext[s].at[block], ext[s].at[block], src_sem.at[0], ext_sem.at[s, block], core).wait_recv()

    def forward_copy(s, i, block):
        return rcopy(ext[s].at[block], ext[s].at[block], fwd_sem.at[s, i], ext_sem.at[s, block], core)

    def missing(i):
        return no_left if i == 0 else no_right

    def land(s):
        for i in (0, 1):

            @pl.when(is_owner)
            def _():
                ext_wait(s, 1 + i)
                forward_copy(s, i, 1 + i).start()

            @pl.when(jnp.logical_and(not_owner, jnp.logical_not(missing(i))))
            def _():
                ext_wait(s, 3 * i)
                forward_copy(s, i, 3 * i).start()

    def arrive(s):
        for i in (0, 1):

            @pl.when(not_owner)
            def _():
                ext_wait(s, 1 + i)

            @pl.when(jnp.logical_and(is_owner, jnp.logical_not(missing(i))))
            def _():
                ext_wait(s, 3 * i)

    lane = lax.broadcasted_iota(jnp.int32, (1, HALO), 1)

    def place_of(tile_no, which):
        mine = tile_no == c
        top = jnp.where(mine, pos_ref[which, 0], posn[which, 0])
        left = jnp.where(mine, pos_ref[which, 1], posn[which, 1])
        return top, left // HALO, lax.rem(left, HALO)

    def cut(s, spot):
        top, block, rem = spot
        back = lax.rem(HALO - rem, HALO)
        for part in (0, 1):
            for j in (0, 1):
                near = ext[s][block + j, part, pl.ds(top, n), :]
                far = ext[s][block + j + 1, part, pl.ds(top, n), :]
                mixed = jnp.where(lane >= rem, near, far)
                win[s, part, :, j * HALO : (j + 1) * HALO] = pltpu.roll(mixed, back, 1)

    @pl.when(d == 1)
    def _():
        land(1)

    land(0)
    for item in loads:
        item.wait()
    pos_copy.wait()

    @pl.when(c == m)
    def _():
        pltpu.make_async_copy(probe_ref.at[0], psi0, probe_sem.at[2]).wait()

    @pl.when(c != m)
    def _():
        probe_copy.wait_recv()

    spot = place_of(d, m)
    arrive(0)
    cut(0, spot)
    wr, wi = win[0, 0], win[0, 1]
    pr, pi = psi0[0], psi0[1]
    spec_r, spec_i = transform(pr * wr - pi * wi, pr * wi + pi * wr, tab, 0, 1)
    hr, hi = prop[0], prop[1]
    wave_r, wave_i = transform(spec_r * hr - spec_i * hi, spec_r * hi + spec_i * hr, tab, 1, 0)
    psi1[0] = wave_r
    psi1[1] = wave_i

    @pl.when(d == 0)
    def _():
        land(1)

    arrive(1)
    cut(1, spot)
    wr, wi = win[1, 0], win[1, 1]
    wave_r, wave_i = psi1[0], psi1[1]
    far_r, far_i = transform(wave_r * wr - wave_i * wi, wave_r * wi + wave_i * wr, tab, 0, 1)
    mine_int[...] = far_r * far_r + far_i * far_i
    int_copy = rcopy(mine_int, their_int, int_sem.at[0], int_sem.at[1], core)
    int_copy.start()

    @pl.when(is_owner)
    def _():
        meas_local.wait()

    @pl.when(not_owner)
    def _():
        meas_copy.wait_recv()

    int_copy.wait()
    resid = mine_int[...] + their_int[...] - pattern[...]
    q_r, q_i = transform(resid * far_r, resid * far_i, tab, 1, 0)

    v_copy = rcopy(vsend, vrecv, v_sem.at[0], v_sem.at[1], core)

    def store_window(ref, start, real, imag):
        for j in (0, 1):
            cols = slice(j * HALO, (j + 1) * HALO)
            ref[j, 0, :, :] = real[:, cols]
            ref[j, 1, :, :] = imag[:, cols]

    def window_at(tile_no, which):
        return spread.at[tile_no, which, 3:5, :, room : room + n, :]

    def keep(real, imag):
        store_window(window_at(d, m), 0, real, imag)

    def to_across():
        return rcopy(window_at(d, m), window_at(d, m), w_send.at[0], w_recv.at[0], across)

    def to_beside(which_tile, k):
        return rcopy(window_at(which_tile, m), window_at(which_tile, m), w_send.at[k], w_recv.at[k], beside)

    def finish():
        v_copy.wait_recv()
        here = window_at(d, m)
        here[...] = here[...] + vrecv[...]

        @pl.when(is_owner)
        def _():
            to_beside(d, 1).start()

        @pl.when(not_owner)
        def _():
            to_across().start()

    wr, wi = win[1, 0], win[1, 1]
    wave_r, wave_i = psi1[0], psi1[1]
    v_r = wave_r * q_r + wave_i * q_i
    v_i = wave_r * q_i - wave_i * q_r

    @pl.when(c == 0)
    def _():
        store_window(vsend, 0, v_r, v_i)
        v_copy.start()

    @pl.when(c == 1)
    def _():
        keep(v_r, v_i)

    spec_r, spec_i = transform(wr * q_r + wi * q_i, wr * q_i - wi * q_r, tab, 0, 1)

    @pl.when(c == 1)
    def _():
        finish()

    hr, hi = prop[0], prop[1]
    q_r, q_i = transform(spec_r * hr + spec_i * hi, spec_i * hr - spec_r * hi, tab, 1, 0)
    pr, pi = psi0[0], psi0[1]
    v_r = pr * q_r + pi * q_i
    v_i = pr * q_i - pi * q_r

    @pl.when(c == 1)
    def _():
        store_window(vsend, 0, v_r, v_i)
        v_copy.start()

    @pl.when(c == 0)
    def _():
        keep(v_r, v_i)
        finish()

    def placed(tile_no, which, block, part):
        top, first, rem = place_of(tile_no, which)
        at = block - first + 3
        near = spread[tile_no, which, at, part, pl.ds(room - top, rows), :]
        far = spread[tile_no, which, at - 1, part, pl.ds(room - top, rows), :]
        return pltpu.roll(jnp.where(lane < HALO - rem, near, far), rem, 1)

    def gather_block(block):
        for part in (0, 1):
            terms = []
            for tile_no in (0, 1):
                local = block - 2 * tile_no
                if 0 <= local < 4:
                    for which in (0, 1):
                        terms.append(placed(tile_no, which, local, part))
            accum[block, part] = functools.reduce(jnp.add, terms)

    def rim_copy(side):
        return rcopy(
            accum.at[5 * side],
            rim.at[1 - side],
            rim_send.at[side],
            rim_recv.at[1 - side],
            {"tile": t - 2 + 4 * side},
        )

    def out_copy(half):
        block = 1 + 2 * (1 - d) + half
        return rcopy(
            accum.at[block],
            out_ref.at[0, :, :, half * HALO : (half + 1) * HALO],
            out_send.at[half],
            out_recv.at[half],
            core,
        )

    has_low = z > 0
    has_high = z < pairs - 1

    @pl.when(is_owner)
    def _():
        arrived = rcopy(window_at(1 - d, m), window_at(1 - d, m), w_send.at[2], w_recv.at[0], across)
        arrived.wait_recv()
        to_beside(1 - d, 2).start()
        rcopy(window_at(d, 1 - m), window_at(d, 1 - m), w_send.at[1], w_recv.at[1], beside).wait_recv()
        rcopy(window_at(1 - d, 1 - m), window_at(1 - d, 1 - m), w_send.at[2], w_recv.at[2], beside).wait_recv()
        gather_block(0)

        @pl.when(has_low)
        def _():
            rim_copy(0).start()

        gather_block(5)

        @pl.when(has_high)
        def _():
            rim_copy(1).start()

        for block in (1, 2, 3, 4):
            gather_block(block)

        @pl.when(has_low)
        def _():
            rcopy(rim.at[0], rim.at[0], rim_send.at[0], rim_recv.at[0], core).wait_recv()
            accum[1] = accum[1] + rim[0]

        @pl.when(has_high)
        def _():
            rcopy(rim.at[1], rim.at[1], rim_send.at[1], rim_recv.at[1], core).wait_recv()
            accum[4] = accum[4] + rim[1]

        for half in (0, 1):
            out_copy(half).start()
        for half in (0, 1):
            out_ref[0, :, :, half * HALO : (half + 1) * HALO] = accum[1 + 2 * d + half]
        for half in (0, 1):
            out_copy(half).wait_send()
        to_beside(d, 1).wait_send()
        to_beside(1 - d, 2).wait_send()

        @pl.when(has_low)
        def _():
            rim_copy(0).wait_send()

        @pl.when(has_high)
        def _():
            rim_copy(1).wait_send()

        meas_copy.wait_send()

    @pl.when(not_owner)
    def _():
        to_across().wait_send()
        for half in (0, 1):
            out_copy(half).wait_recv()

    v_copy.wait_send()

    @pl.when(c == m)
    def _():
        probe_copy.wait_send()

    def placed_done(src, block, send, depth):
        @pl.when(d != depth)
        def _():
            rcopy(src, ext_near.at[block], send, ext_sem.at[0, block], across).wait_send()

    placed_done(half_of(0), 1, src_sem.at[0], c)
    placed_done(half_of(1), 2, src_sem.at[1], c)
    placed_done(half_of(1 - c), inner_block, src_sem.at[2], 1 - c)

    @pl.when(has_outer)
    def _():
        outer_copy(0).wait_send()

    for s in (0, 1):
        for i in (0, 1):

            @pl.when(is_owner)
            def _():
                forward_copy(s, i, 1 + i).wait_send()

            @pl.when(jnp.logical_and(not_owner, jnp.logical_not(missing(i))))
            def _():
                forward_copy(s, i, 3 * i).wait_send()


def body(pairs, probe, object_slices, positions, measured):
    n = probe.shape[-1]
    rows = object_slices.shape[2]
    room = rows - n
    f32 = jnp.float32
    tables = jnp.asarray(dft_tables(n))
    transfer = jnp.asarray(propagator(n))
    vmem = pl.BlockSpec(memory_space=pltpu.VMEM)
    anywhere = pl.BlockSpec(memory_space=pl.ANY)
    dma = pltpu.SemaphoreType.DMA
    return pl.pallas_call(
        functools.partial(kernel, pairs),
        out_shape=jax.ShapeDtypeStruct(object_slices.shape, f32),
        in_specs=[vmem, vmem, pl.BlockSpec(memory_space=pltpu.SMEM), vmem, anywhere, anywhere],
        out_specs=vmem,
        scratch_shapes=[
            pltpu.VMEM((5, 2, rows, HALO), f32),
            pltpu.VMEM((5, 2, rows, HALO), f32),
            pltpu.VMEM((2, n, n), f32),
            pltpu.VMEM((2, n, n), f32),
            pltpu.VMEM((2, 2, n, n), f32),
            pltpu.VMEM((n, n), f32),
            pltpu.SMEM(positions.shape, jnp.int32),
            pltpu.VMEM(tables.shape, jnp.bfloat16),
            pltpu.VMEM(transfer.shape, f32),
            pltpu.VMEM((n, n), f32),
            pltpu.VMEM((n, n), f32),
            pltpu.VMEM((2, 2, n, HALO), f32),
            pltpu.VMEM((2, 2, n, HALO), f32),
            pltpu.VMEM((2, 2, 7, 2, n + 2 * room, HALO), f32),
            pltpu.VMEM((6, 2, rows, HALO), f32),
            pltpu.VMEM((2, 2, rows, HALO), f32),
            dma((2,)),
            dma((4,)),
            dma((2, 2)),
            dma((2, 4)),
            dma((2,)),
            dma((3,)),
            dma((3,)),
            dma((2,)),
            dma((2,)),
            dma((3,)),
            dma((3,)),
            dma((2,)),
            dma((2,)),
            dma((2,)),
            dma((2,)),
        ],
        compiler_params=pltpu.CompilerParams(
            collective_id=0, has_side_effects=True, vmem_limit_bytes=60 * 1024 * 1024
        ),
    )(probe, object_slices, positions, measured, tables, transfer)


def solution(mesh):
    placed = (
        P("mode", None, None, None),
        P("depth", None, None, "tile"),
        P("tile", None),
        P("tile", None, None),
    )
    pairs = mesh.shape["tile"] // 2
    return jax.shard_map(
        functools.partial(body, pairs),
        mesh=mesh,
        in_specs=placed,
        out_specs=P("depth", None, None, "tile"),
        check_vma=False,
    )
```

profile of v0, /device:TPU:0, one launch (start us, length us, event | category | flops | bytes accessed | tf_op | source)
XLA Modules:
  0.0 67.8 jit_solution(8355367242296448648)
XLA Ops:
  0.0 65.7 %shard_map.64 = f32[1,2,384,256]{3,2,1,0:T(8,128)} custom-call(f32[1,2,256,256]{3,2,1,0:T(8,128)} %probe_ref.1, f32[1,2,384,256]{3,2,1,0:T(8,128)} %obj_ref.1, s32[2,2]{1,0:T(2,128)} %pos_ref.1, f32[2,256,256]{2,1,0:T(8,128)} %meas_ref.1, bf16[2,2,512,512]{3,2,1,0:T(8,128)(2,1)} %constant.4.clone.tab_hbm, f32[2,256,256]{2,1,0:T(8,128)} %constant.5.clone.prop_hbm), custom_call_target="tpu_custom_call" | custom-call | tf_op jit(solution)/shard_map/pallas_call | solution.py:540
  65.7 2.1 %copy.8 = f32[1,2,384,256]{3,2,1,0:T(8,128)} copy(f32[1,2,384,256]{3,2,1,0:T(8,128)} %shard_map.64) | data formatting | bytes 1572864
where the time goes:
time: 68 us; the launch traced here: 67.8 us
  Pallas kernels  65.7 us (97%)
  local copies, waits for them, and re-layouts  2.06 us (3%)
    pallas_call x1, Pallas kernels, body(): pl.pallas_call(functools.partial(kernel, pairs), out_shape=jax.ShapeDtype...  65.7 us
    unnamed x1, local copies, waits for them, and re-layouts  2.06 us

commit v1 on v0

--- a/solution.py
+++ b/solution.py
@@ -78,7 +78,8 @@
     their_int,
     vsend,
     vrecv,
-    spread,
+    spread_r,
+    spread_i,
     accum,
     rim,
     load_sem,
@@ -143,6 +144,7 @@
     pl.semaphore_wait(barrier, peers)
 
     ext = (ext_near, ext_far)
+    spread = (spread_r, spread_i)
 
     def half_of(h):
         return obj_ref.at[0, :, :, pl.ds(pl.multiple_of(h * HALO, HALO), HALO)]
@@ -221,11 +223,12 @@
     def _():
         @pl.loop(0, 4)
         def _(w):
-            for j in (0, 1, 2, 5, 6):
-                spread[w // 2, lax.rem(w, 2), j] = jnp.zeros(spread.shape[3:], jnp.float32)
-            for j in (3, 4):
-                for edge in (0, room + n):
-                    spread[w // 2, lax.rem(w, 2), j, :, edge : edge + room, :] = jnp.zeros((2, room, HALO), jnp.float32)
+            for field in spread:
+                for j in (0, 1, 2, 5, 6):
+                    field[w // 2, lax.rem(w, 2), j] = jnp.zeros(field.shape[3:], jnp.float32)
+                for j in (3, 4):
+                    for edge in (0, room + n):
+                        field[w // 2, lax.rem(w, 2), j, edge : edge + room, :] = jnp.zeros((room, HALO), jnp.float32)
 
     def ext_wait(s, block):
         rcopy(ext[s].at[block], ext[s].at[block], src_sem.at[0], ext_sem.at[s, block], core).wait_recv()
@@ -331,38 +334,57 @@
     resid = mine_int[...] + their_int[...] - pattern[...]
     q_r, q_i = transform(resid * far_r, resid * far_i, tab, 1, 0)
 
-    v_copy = rcopy(vsend, vrecv, v_sem.at[0], v_sem.at[1], core)
-
-    def store_window(ref, start, real, imag):
-        for j in (0, 1):
-            cols = slice(j * HALO, (j + 1) * HALO)
-            ref[j, 0, :, :] = real[:, cols]
-            ref[j, 1, :, :] = imag[:, cols]
-
-    def window_at(tile_no, which):
-        return spread.at[tile_no, which, 3:5, :, room : room + n, :]
+    def v_copy(part):
+        return rcopy(vsend.at[part], vrecv.at[part], v_sem.at[0, part], v_sem.at[1, part], core)
+
+    def window_at(tile_no, which, part):
+        return spread[part].at[tile_no, which, 3:5, room : room + n, :]
+
+    def give(real, imag):
+        for part, value in enumerate((real, imag)):
+            for j in (0, 1):
+                vsend[part, j] = value[:, j * HALO : (j + 1) * HALO]
+            v_copy(part).start()
 
     def keep(real, imag):
-        store_window(window_at(d, m), 0, real, imag)
-
-    def to_across():
-        return rcopy(window_at(d, m), window_at(d, m), w_send.at[0], w_recv.at[0], across)
-
-    def to_beside(which_tile, k):
-        return rcopy(window_at(which_tile, m), window_at(which_tile, m), w_send.at[k], w_recv.at[k], beside)
+        for part, value in enumerate((real, imag)):
+            for j in (0, 1):
+                spread[part][d, m, 3 + j, room : room + n, :] = value[:, j * HALO : (j + 1) * HALO]
+
+    def carry(tile_no, which, part, k, j, target):
+        ref = window_at(tile_no, which, part)
+        return rcopy(ref, ref, w_send.at[k, part], w_recv.at[j, part], target)
+
+    def to_across(part):
+        return carry(d, m, part, 0, 0, across)
+
+    def to_beside(part):
+        return carry(d, m, part, 1, 1, beside)
+
+    def aside():
+        return carry(d, m, 1, 1, 3, beside)
+
+    def relay_beside():
+        return carry(1 - d, m, 0, 2, 2, beside)
+
+    def relay_across():
+        return carry(d, 1 - m, 1, 2, 2, across)
 
     def finish():
-        v_copy.wait_recv()
-        here = window_at(d, m)
-        here[...] = here[...] + vrecv[...]
-
-        @pl.when(is_owner)
-        def _():
-            to_beside(d, 1).start()
-
-        @pl.when(not_owner)
-        def _():
-            to_across().start()
+        for part in (0, 1):
+            v_copy(part).wait_recv()
+            here = window_at(d, m, part)
+            here[...] = here[...] + vrecv[part]
+
+            @pl.when(is_owner)
+            def _():
+                to_beside(part).start()
+
+            @pl.when(not_owner)
+            def _():
+                if part == 1:
+                    aside().start()
+                to_across(part).start()
 
     wr, wi = win[1, 0], win[1, 1]
     wave_r, wave_i = psi1[0], psi1[1]
@@ -371,8 +393,7 @@
 
     @pl.when(c == 0)
     def _():
-        store_window(vsend, 0, v_r, v_i)
-        v_copy.start()
+        give(v_r, v_i)
 
     @pl.when(c == 1)
     def _():
@@ -392,8 +413,7 @@
 
     @pl.when(c == 1)
     def _():
-        store_window(vsend, 0, v_r, v_i)
-        v_copy.start()
+        give(v_r, v_i)
 
     @pl.when(c == 0)
     def _():
@@ -403,36 +423,36 @@
     def placed(tile_no, which, block, part):
         top, first, rem = place_of(tile_no, which)
         at = block - first + 3
-        near = spread[tile_no, which, at, part, pl.ds(room - top, rows), :]
-        far = spread[tile_no, which, at - 1, part, pl.ds(room - top, rows), :]
+        near = spread[part][tile_no, which, at, pl.ds(room - top, rows), :]
+        far = spread[part][tile_no, which, at - 1, pl.ds(room - top, rows), :]
         return pltpu.roll(jnp.where(lane < HALO - rem, near, far), rem, 1)
 
-    def gather_block(block):
-        for part in (0, 1):
-            terms = []
-            for tile_no in (0, 1):
-                local = block - 2 * tile_no
-                if 0 <= local < 4:
-                    for which in (0, 1):
-                        terms.append(placed(tile_no, which, local, part))
-            accum[block, part] = functools.reduce(jnp.add, terms)
-
-    def rim_copy(side):
+    def gather_block(block, part):
+        terms = []
+        for tile_no in (0, 1):
+            local = block - 2 * tile_no
+            if 0 <= local < 4:
+                for which in (0, 1):
+                    terms.append(placed(tile_no, which, local, part))
+        accum[block, part] = functools.reduce(jnp.add, terms)
+
+    def rim_copy(side, part):
         return rcopy(
-            accum.at[5 * side],
-            rim.at[1 - side],
-            rim_send.at[side],
-            rim_recv.at[1 - side],
+            accum.at[5 * side, part],
+            rim.at[1 - side, part],
+            rim_send.at[side, part],
+            rim_recv.at[1 - side, part],
             {"tile": t - 2 + 4 * side},
         )
 
-    def out_copy(half):
-        block = 1 + 2 * (1 - d) + half
+    def out_copy(outer, part):
+        half = d * (1 - outer) + (1 - d) * outer
+        block = 3 - 2 * d + half
         return rcopy(
-            accum.at[block],
-            out_ref.at[0, :, :, half * HALO : (half + 1) * HALO],
-            out_send.at[half],
-            out_recv.at[half],
+            accum.at[block, part],
+            out_ref.at[0, part, :, pl.ds(pl.multiple_of(half * HALO, HALO), HALO)],
+            out_send.at[outer, part],
+            out_recv.at[outer, part],
             core,
         )
 
@@ -441,62 +461,70 @@
 
     @pl.when(is_owner)
     def _():
-        arrived = rcopy(window_at(1 - d, m), window_at(1 - d, m), w_send.at[2], w_recv.at[0], across)
-        arrived.wait_recv()
-        to_beside(1 - d, 2).start()
-        rcopy(window_at(d, 1 - m), window_at(d, 1 - m), w_send.at[1], w_recv.at[1], beside).wait_recv()
-        rcopy(window_at(1 - d, 1 - m), window_at(1 - d, 1 - m), w_send.at[2], w_recv.at[2], beside).wait_recv()
-        gather_block(0)
-
-        @pl.when(has_low)
-        def _():
-            rim_copy(0).start()
-
-        gather_block(5)
-
-        @pl.when(has_high)
-        def _():
-            rim_copy(1).start()
-
-        for block in (1, 2, 3, 4):
-            gather_block(block)
-
-        @pl.when(has_low)
-        def _():
-            rcopy(rim.at[0], rim.at[0], rim_send.at[0], rim_recv.at[0], core).wait_recv()
-            accum[1] = accum[1] + rim[0]
-
-        @pl.when(has_high)
-        def _():
-            rcopy(rim.at[1], rim.at[1], rim_send.at[1], rim_recv.at[1], core).wait_recv()
-            accum[4] = accum[4] + rim[1]
-
-        for half in (0, 1):
-            out_copy(half).start()
-        for half in (0, 1):
-            out_ref[0, :, :, half * HALO : (half + 1) * HALO] = accum[1 + 2 * d + half]
-        for half in (0, 1):
-            out_copy(half).wait_send()
-        to_beside(d, 1).wait_send()
-        to_beside(1 - d, 2).wait_send()
-
-        @pl.when(has_low)
-        def _():
-            rim_copy(0).wait_send()
-
-        @pl.when(has_high)
-        def _():
-            rim_copy(1).wait_send()
+        carry(1 - d, m, 0, 2, 0, across).wait_recv()
+        relay_beside().start()
+        for part in (0, 1):
+            if part == 1:
+                carry(1 - d, m, 1, 2, 0, across).wait_recv()
+            carry(d, 1 - m, part, 2, 1, beside).wait_recv()
+            carry(1 - d, 1 - m, part, 2, 2, beside).wait_recv()
+            gather_block(0, part)
+
+            @pl.when(has_low)
+            def _():
+                rim_copy(0, part).start()
+
+            gather_block(5, part)
+
+            @pl.when(has_high)
+            def _():
+                rim_copy(1, part).start()
+
+            for block in (2, 3):
+                gather_block(block, part)
+            out_copy(0, part).start()
+            for block in (1, 4):
+                gather_block(block, part)
+        for part in (0, 1):
+            for side, block, there in ((0, 1, has_low), (1, 4, has_high)):
+
+                @pl.when(there)
+                def _():
+                    rcopy(
+                        rim.at[side, part], rim.at[side, part], rim_send.at[side, part], rim_recv.at[side, part], core
+                    ).wait_recv()
+                    accum[block, part] = accum[block, part] + rim[side, part]
+
+            out_copy(1, part).start()
+            for half in (0, 1):
+                out_ref[0, part, :, half * HALO : (half + 1) * HALO] = accum[1 + 2 * d + half, part]
+        relay_beside().wait_send()
+        for part in (0, 1):
+            to_beside(part).wait_send()
+            for outer in (0, 1):
+                out_copy(outer, part).wait_send()
+            for side, there in ((0, has_low), (1, has_high)):
+
+                @pl.when(there)
+                def _():
+                    rim_copy(side, part).wait_send()
 
         meas_copy.wait_send()
 
     @pl.when(not_owner)
     def _():
-        to_across().wait_send()
-        for half in (0, 1):
-            out_copy(half).wait_recv()
-
-    v_copy.wait_send()
+        carry(d, 1 - m, 1, 2, 3, beside).wait_recv()
+        relay_across().start()
+        for part in (0, 1):
+            to_across(part).wait_send()
+        aside().wait_send()
+        relay_across().wait_send()
+        for part in (0, 1):
+            for outer in (0, 1):
+                out_copy(outer, part).wait_recv()
+
+    for part in (0, 1):
+        v_copy(part).wait_send()
 
     @pl.when(c == m)
     def _():
@@ -556,7 +584,8 @@
             pltpu.VMEM((n, n), f32),
             pltpu.VMEM((2, 2, n, HALO), f32),
             pltpu.VMEM((2, 2, n, HALO), f32),
-            pltpu.VMEM((2, 2, 7, 2, n + 2 * room, HALO), f32),
+            pltpu.VMEM((2, 2, 7, n + 2 * room, HALO), f32),
+            pltpu.VMEM((2, 2, 7, n + 2 * room, HALO), f32),
             pltpu.VMEM((6, 2, rows, HALO), f32),
             pltpu.VMEM((2, 2, rows, HALO), f32),
             dma((2,)),
@@ -567,13 +596,13 @@
             dma((3,)),
             dma((3,)),
             dma((2,)),
-            dma((2,)),
-            dma((3,)),
-            dma((3,)),
-            dma((2,)),
-            dma((2,)),
-            dma((2,)),
-            dma((2,)),
+            dma((2, 2)),
+            dma((3, 2)),
+            dma((4, 2)),
+            dma((2, 2)),
+            dma((2, 2)),
+            dma((2, 2)),
+            dma((2, 2)),
         ],
         compiler_params=pltpu.CompilerParams(
             collective_id=0, has_side_effects=True, vmem_limit_bytes=60 * 1024 * 1024

time: 68 us -> 62.2 us (0.915)
  Pallas kernels: 65.7 us -> 60 us
    pallas_call x1, Pallas kernels: 65.7 us -> 60 us  [body(): pl.pallas_call(functools.partial(kernel, pairs), out_shape=jax.ShapeDtype...]
where the time goes in v1:
time: 62.2 us; the launch traced here: 62.1 us
  Pallas kernels  60 us (96%)
  local copies, waits for them, and re-layouts  2.06 us (3%)
    pallas_call x1, Pallas kernels, body(): pl.pallas_call(functools.partial(kernel, pairs), out_shape=jax.ShapeDtype...  60 us
    unnamed x1, local copies, waits for them, and re-layouts  2.06 us

profile of v1, /device:TPU:0, one launch (start us, length us, event | category | flops | bytes accessed | tf_op | source)
XLA Modules:
  0.0 62.1 jit_solution(4024693399893216240)
XLA Ops:
  0.0 60.0 %shard_map.64 = f32[1,2,384,256]{3,2,1,0:T(8,128)} custom-call(f32[1,2,256,256]{3,2,1,0:T(8,128)} %probe_ref.1, f32[1,2,384,256]{3,2,1,0:T(8,128)} %obj_ref.1, s32[2,2]{1,0:T(2,128)} %pos_ref.1, f32[2,256,256]{2,1,0:T(8,128)} %meas_ref.1, bf16[2,2,512,512]{3,2,1,0:T(8,128)(2,1)} %constant.4.clone.tab_hbm, f32[2,256,256]{2,1,0:T(8,128)} %constant.5.clone.prop_hbm), custom_call_target="tpu_custom_call" | custom-call | tf_op jit(solution)/shard_map/pallas_call | solution.py:568
  60.0 2.1 %copy.8 = f32[1,2,384,256]{3,2,1,0:T(8,128)} copy(f32[1,2,384,256]{3,2,1,0:T(8,128)} %shard_map.64) | data formatting | bytes 1572864

commit v2 on v1

--- a/solution.py
+++ b/solution.py
@@ -85,6 +85,7 @@
     load_sem,
     src_sem,
     fwd_sem,
+    relay_sem,
     ext_sem,
     pos_sem,
     probe_sem,
@@ -146,47 +147,55 @@
     ext = (ext_near, ext_far)
     spread = (spread_r, spread_i)
 
-    def half_of(h):
-        return obj_ref.at[0, :, :, pl.ds(pl.multiple_of(h * HALO, HALO), HALO)]
-
-    def place(src, block, send, depth):
+    tall = rows // 2
+
+    def strip(r):
+        return pl.ds(pl.multiple_of(r * tall, 8), tall)
+
+    def half_of(h, r):
+        return obj_ref.at[0, :, strip(r), pl.ds(pl.multiple_of(h * HALO, HALO), HALO)]
+
+    def slot(s, block, r):
+        return ext[s].at[block, :, strip(r), :]
+
+    def place(h, block, send, depth):
         for s in (0, 1):
-            dst = ext[s].at[block]
-            sem = ext_sem.at[s, block]
 
             @pl.when(jnp.logical_and(d == s, depth == s))
             def _():
-                pltpu.make_async_copy(src, dst, sem).start()
+                for r in (0, 1):
+                    pltpu.make_async_copy(half_of(h, r), slot(s, block, r), ext_sem.at[s, block, r]).start()
 
             @pl.when(jnp.logical_and(d == s, depth != s))
             def _():
-                rcopy(src, dst, send, sem, across).start()
+                rcopy(half_of(h, m), slot(s, block, m), send, ext_sem.at[s, block, m], across).start()
 
     inner_block = 3 * c
     outer_block = 3 - 3 * c
     outer_tile = t - 2 + 4 * c
     has_outer = jnp.logical_or(jnp.logical_and(c == 0, z > 0), jnp.logical_and(c == 1, z < pairs - 1))
 
-    def outer_copy(s):
+    def outer_copy(s, r):
         return rcopy(
-            half_of(c),
-            ext[s].at[outer_block],
-            src_sem.at[3],
-            ext_sem.at[s, outer_block],
+            half_of(c, r),
+            slot(s, outer_block, r),
+            src_sem.at[3 + r],
+            ext_sem.at[s, outer_block, r],
             {"depth": 1 - c, "tile": outer_tile},
         )
 
     pos_copy = rcopy(pos_ref, posn, pos_sem.at[0], pos_sem.at[1], core)
     pos_copy.start()
-    place(half_of(0), 1, src_sem.at[0], c)
-    place(half_of(1), 2, src_sem.at[1], c)
-    place(half_of(1 - c), inner_block, src_sem.at[2], 1 - c)
+    place(0, 1, src_sem.at[0], c)
+    place(1, 2, src_sem.at[1], c)
+    place(1 - c, inner_block, src_sem.at[2], 1 - c)
 
     for s in (0, 1):
 
         @pl.when(jnp.logical_and(has_outer, d == s))
         def _():
-            outer_copy(s).start()
+            for r in (0, 1):
+                outer_copy(s, r).start()
 
     probe_copy = rcopy(probe_ref.at[0], psi0, probe_sem.at[0], probe_sem.at[1], beside)
 
@@ -230,38 +239,62 @@
                     for edge in (0, room + n):
                         field[w // 2, lax.rem(w, 2), j, edge : edge + room, :] = jnp.zeros((room, HALO), jnp.float32)
 
-    def ext_wait(s, block):
-        rcopy(ext[s].at[block], ext[s].at[block], src_sem.at[0], ext_sem.at[s, block], core).wait_recv()
-
-    def forward_copy(s, i, block):
-        return rcopy(ext[s].at[block], ext[s].at[block], fwd_sem.at[s, i], ext_sem.at[s, block], core)
+    def ext_wait(s, block, r):
+        ref = slot(s, block, r)
+        rcopy(ref, ref, src_sem.at[0], ext_sem.at[s, block, r], core).wait_recv()
+
+    def forward_copy(s, i, block, r):
+        ref = slot(s, block, r)
+        return rcopy(ref, ref, fwd_sem.at[s, i, r], ext_sem.at[s, block, r], core)
+
+    def relay_copy(s, i, block):
+        ref = slot(s, block, m)
+        return rcopy(ref, ref, relay_sem.at[s, i], ext_sem.at[s, block, m], beside)
 
     def missing(i):
         return no_left if i == 0 else no_right
 
-    def land(s):
+    def lands(i):
+        return jnp.logical_and(not_owner, jnp.logical_not(missing(i)))
+
+    def relays(s, i):
+        return jnp.logical_and(d != s, jnp.logical_and(not_owner, d != i))
+
+    def land(s, second):
+        r = 1 - m if second else m
         for i in (0, 1):
 
             @pl.when(is_owner)
             def _():
-                ext_wait(s, 1 + i)
-                forward_copy(s, i, 1 + i).start()
-
-            @pl.when(jnp.logical_and(not_owner, jnp.logical_not(missing(i))))
-            def _():
-                ext_wait(s, 3 * i)
-                forward_copy(s, i, 3 * i).start()
+                ext_wait(s, 1 + i, r)
+                forward_copy(s, i, 1 + i, r).start()
+
+            @pl.when(lands(i))
+            def _():
+                ext_wait(s, 3 * i, r)
+                forward_copy(s, i, 3 * i, r).start()
+
+            if not second:
+
+                @pl.when(jnp.logical_and(is_owner, d != s))
+                def _():
+                    relay_copy(s, i, 1 + i).start()
+
+                @pl.when(relays(s, i))
+                def _():
+                    relay_copy(s, i, 3 * i).start()
 
     def arrive(s):
         for i in (0, 1):
-
-            @pl.when(not_owner)
-            def _():
-                ext_wait(s, 1 + i)
-
-            @pl.when(jnp.logical_and(is_owner, jnp.logical_not(missing(i))))
-            def _():
-                ext_wait(s, 3 * i)
+            for r in (0, 1):
+
+                @pl.when(not_owner)
+                def _():
+                    ext_wait(s, 1 + i, r)
+
+                @pl.when(jnp.logical_and(is_owner, jnp.logical_not(missing(i))))
+                def _():
+                    ext_wait(s, 3 * i, r)
 
     lane = lax.broadcasted_iota(jnp.int32, (1, HALO), 1)
 
@@ -283,9 +316,16 @@
 
     @pl.when(d == 1)
     def _():
-        land(1)
-
-    land(0)
+        land(1, False)
+        land(1, True)
+
+    land(0, False)
+    land(0, True)
+
+    @pl.when(d == 0)
+    def _():
+        land(1, False)
+
     for item in loads:
         item.wait()
     pos_copy.wait()
@@ -311,7 +351,7 @@
 
     @pl.when(d == 0)
     def _():
-        land(1)
+        land(1, True)
 
     arrive(1)
     cut(1, spot)
@@ -530,29 +570,40 @@
     def _():
         probe_copy.wait_send()
 
-    def placed_done(src, block, send, depth):
+    def placed_done(h, block, send, depth):
         @pl.when(d != depth)
         def _():
-            rcopy(src, ext_near.at[block], send, ext_sem.at[0, block], across).wait_send()
-
-    placed_done(half_of(0), 1, src_sem.at[0], c)
-    placed_done(half_of(1), 2, src_sem.at[1], c)
-    placed_done(half_of(1 - c), inner_block, src_sem.at[2], 1 - c)
+            rcopy(half_of(h, m), slot(0, block, m), send, ext_sem.at[0, block, m], across).wait_send()
+
+    placed_done(0, 1, src_sem.at[0], c)
+    placed_done(1, 2, src_sem.at[1], c)
+    placed_done(1 - c, inner_block, src_sem.at[2], 1 - c)
 
     @pl.when(has_outer)
     def _():
-        outer_copy(0).wait_send()
+        for r in (0, 1):
+            outer_copy(0, r).wait_send()
 
     for s in (0, 1):
         for i in (0, 1):
 
             @pl.when(is_owner)
             def _():
-                forward_copy(s, i, 1 + i).wait_send()
-
-            @pl.when(jnp.logical_and(not_owner, jnp.logical_not(missing(i))))
-            def _():
-                forward_copy(s, i, 3 * i).wait_send()
+                for r in (0, 1):
+                    forward_copy(s, i, 1 + i, r).wait_send()
+
+            @pl.when(lands(i))
+            def _():
+                for r in (0, 1):
+                    forward_copy(s, i, 3 * i, r).wait_send()
+
+            @pl.when(jnp.logical_and(is_owner, d != s))
+            def _():
+                relay_copy(s, i, 1 + i).wait_send()
+
+            @pl.when(relays(s, i))
+            def _():
+                relay_copy(s, i, 3 * i).wait_send()
 
 
 def body(pairs, probe, object_slices, positions, measured):
@@ -589,9 +640,10 @@
             pltpu.VMEM((6, 2, rows, HALO), f32),
             pltpu.VMEM((2, 2, rows, HALO), f32),
             dma((2,)),
-            dma((4,)),
+            dma((5,)),
+            dma((2, 2, 2)),
             dma((2, 2)),
-            dma((2, 4)),
+            dma((2, 4, 2)),
             dma((2,)),
             dma((3,)),
             dma((3,)),

time: 62.2 us -> 61.8 us (level)
  no operation moved by 1% of the time
where the time goes in v2:
time: 61.8 us; the launch traced here: 61.6 us
  Pallas kernels  59.5 us (96%)
  local copies, waits for them, and re-layouts  2.06 us (3%)
    pallas_call x1, Pallas kernels, body(): pl.pallas_call(functools.partial(kernel, pairs), out_shape=jax.ShapeDtype...  59.5 us
    unnamed x1, local copies, waits for them, and re-layouts  2.06 us

profile of v2, /device:TPU:0, one launch (start us, length us, event | category | flops | bytes accessed | tf_op | source)
XLA Modules:
  0.0 61.6 jit_solution(1359590460581025780)
XLA Ops:
  0.0 59.5 %shard_map.64 = f32[1,2,384,256]{3,2,1,0:T(8,128)} custom-call(f32[1,2,256,256]{3,2,1,0:T(8,128)} %probe_ref.1, f32[1,2,384,256]{3,2,1,0:T(8,128)} %obj_ref.1, s32[2,2]{1,0:T(2,128)} %pos_ref.1, f32[2,256,256]{2,1,0:T(8,128)} %meas_ref.1, bf16[2,2,512,512]{3,2,1,0:T(8,128)(2,1)} %constant.4.clone.tab_hbm, f32[2,256,256]{2,1,0:T(8,128)} %constant.5.clone.prop_hbm), custom_call_target="tpu_custom_call" | custom-call | tf_op jit(solution)/shard_map/pallas_call | solution.py:619
  59.5 2.1 %copy.8 = f32[1,2,384,256]{3,2,1,0:T(8,128)} copy(f32[1,2,384,256]{3,2,1,0:T(8,128)} %shard_map.64) | data formatting | bytes 1572864

commit v3 on v2

--- a/solution.py
+++ b/solution.py
@@ -98,6 +98,7 @@
     rim_recv,
     out_send,
     out_recv,
+    own_sem,
 ):
     n = psi0.shape[1]
     rows = obj_ref.shape[2]
@@ -496,6 +497,14 @@
             core,
         )
 
+    def own_copy(outer, part):
+        half = (1 - d) * (1 - outer) + d * outer
+        return pltpu.make_async_copy(
+            accum.at[1 + 2 * d + half, part],
+            out_ref.at[0, part, :, pl.ds(pl.multiple_of(half * HALO, HALO), HALO)],
+            own_sem.at[outer, part],
+        )
+
     has_low = z > 0
     has_high = z < pairs - 1
 
@@ -523,6 +532,7 @@
             for block in (2, 3):
                 gather_block(block, part)
             out_copy(0, part).start()
+            own_copy(0, part).start()
             for block in (1, 4):
                 gather_block(block, part)
         for part in (0, 1):
@@ -536,13 +546,13 @@
                     accum[block, part] = accum[block, part] + rim[side, part]
 
             out_copy(1, part).start()
-            for half in (0, 1):
-                out_ref[0, part, :, half * HALO : (half + 1) * HALO] = accum[1 + 2 * d + half, part]
+            own_copy(1, part).start()
         relay_beside().wait_send()
         for part in (0, 1):
             to_beside(part).wait_send()
             for outer in (0, 1):
                 out_copy(outer, part).wait_send()
+                own_copy(outer, part).wait()
             for side, there in ((0, has_low), (1, has_high)):
 
                 @pl.when(there)
@@ -620,7 +630,7 @@
         functools.partial(kernel, pairs),
         out_shape=jax.ShapeDtypeStruct(object_slices.shape, f32),
         in_specs=[vmem, vmem, pl.BlockSpec(memory_space=pltpu.SMEM), vmem, anywhere, anywhere],
-        out_specs=vmem,
+        out_specs=anywhere,
         scratch_shapes=[
             pltpu.VMEM((5, 2, rows, HALO), f32),
             pltpu.VMEM((5, 2, rows, HALO), f32),
@@ -655,6 +665,7 @@
             dma((2, 2)),
             dma((2, 2)),
             dma((2, 2)),
+            dma((2, 2)),
         ],
         compiler_params=pltpu.CompilerParams(
             collective_id=0, has_side_effects=True, vmem_limit_bytes=60 * 1024 * 1024

time: 61.8 us -> 61.1 us (0.989)
  Pallas kernels: 59.5 us -> 58.8 us
    pallas_call x1, Pallas kernels: 59.5 us -> 58.8 us  [body(): pl.pallas_call(functools.partial(kernel, pairs), out_shape=jax.ShapeDtype...]
where the time goes in v3:
time: 61.1 us; the launch traced here: 60.9 us
  Pallas kernels  58.8 us (96%)
  local copies, waits for them, and re-layouts  2.06 us (3%)
    pallas_call x1, Pallas kernels, body(): pl.pallas_call(functools.partial(kernel, pairs), out_shape=jax.ShapeDtype...  58.8 us
    unnamed x1, local copies, waits for them, and re-layouts  2.06 us

profile of v3, /device:TPU:0, one launch (start us, length us, event | category | flops | bytes accessed | tf_op | source)
XLA Modules:
  0.0 60.9 jit_solution(2711806422952423037)
XLA Ops:
  0.0 58.8 %shard_map.64 = f32[1,2,384,256]{3,2,1,0:T(8,128)} custom-call(f32[1,2,256,256]{3,2,1,0:T(8,128)} %probe_ref.1, f32[1,2,384,256]{3,2,1,0:T(8,128)} %obj_ref.1, s32[2,2]{1,0:T(2,128)} %pos_ref.1, f32[2,256,256]{2,1,0:T(8,128)} %meas_ref.1, bf16[2,2,512,512]{3,2,1,0:T(8,128)(2,1)} %constant.4.clone.tab_hbm, f32[2,256,256]{2,1,0:T(8,128)} %constant.5.clone.prop_hbm), custom_call_target="tpu_custom_call" | custom-call | tf_op jit(solution)/shard_map/pallas_call | solution.py:629
  58.8 2.1 %copy.8 = f32[1,2,384,256]{3,2,1,0:T(8,128)} copy(f32[1,2,384,256]{3,2,1,0:T(8,128)} %shard_map.64) | data formatting | bytes 1572864
